TPU v7x, 32 devices: a whole 2x2x4 slice. The times are simulated.
32 devices in a mesh: tract: 2 (over y), sky: 4 (over x, core), band: 4 (over z).
Axes of the slice: x: 2, y: 2, z: 4, core: 2. Of those that a mesh axis runs over, the one named last changes fastest.
Arguments:
- patches: float32 [8, 32, 256, 256], P(('tract', 'band'), 'sky'), parts along dimension 0, may hold values from -6 to 6
- valid_rows: int32 [8, 32], P(('tract', 'band'), 'sky'), parts along dimension 0, may hold values from 64 to 256
- slot_owner: int32 [8, 32, 1], P(('tract', 'band'), 'sky'), parts along dimension 0, may hold values from 0 to 3; in each aligned block of 8 rows (0 to 7, 8 to 15, ..., all dimensions but the last counted through in order) at most 4 rows name the same one
- slot_local: int32 [8, 32], P(('tract', 'band'), 'sky'), parts along dimension 0, may hold values from 0 to 7
- slot_visit: int32 [8, 32], P(('tract', 'band'), 'sky'), parts along dimension 0, may hold values from 0 to 11
- basis_coef: float32 [8, 12, 21], P(('tract', 'band')), parts along dimension 0, may hold values from -1.25 to 1.25
- inv_var: float32 [8, 12], P(('tract', 'band')), parts along dimension 0, may hold values from 0.1 to 1
- kernel_x: bfloat16 [21, 41], replicated, may hold values from -1 to 1
- kernel_y: bfloat16 [21, 41], replicated, may hold values from -1 to 1
Outputs:
- band_coadd: float32 [8, 32, 256, 256], P(('tract', 'band'), 'sky'), parts along dimension 0
- detection: float32 [64, 256, 256], P(('tract', 'sky'), 'band'), parts along dimension 0
There are 2 independent parts, one for each index of `tract`. A program takes and returns all parts, laid end to end along the dimension named above; an argument that names none is the same for every part. Nothing has to cross between parts.
Inputs may be any that keep to these rules, and one draw needn't show every extreme that they name: `slot_owner`: among the pieces of one device no owner appears more than 4 times; some device gives exactly 4 pieces to one owner.
All inputs are finite; a program needn't handle non-finite values.
Results may differ from a plain program's by a relative error of at most 0.015.
Values may be sent and summed in bfloat16 or wider, within the bound.
A program may use at most 128 MiB of HBM per device.

v0:
```python
import functools

import jax
import jax.numpy as jnp
from jax import lax
from jax.experimental import pallas as pl
from jax.experimental.pallas import tpu as pltpu
from jax.sharding import PartitionSpec as P

PATCH_DEV = 8
MESH = pl.DeviceIdType.MESH
F32 = jnp.float32
BF16 = jnp.bfloat16


def band_offsets(bands):
    far_first = sorted(range(1, bands), key=lambda o: -min(o, bands - o))
    return far_first + [0]


def kernel(
    sizes,
    valid_ref,
    owner_ref,
    local_ref,
    visit_ref,
    ivar_ref,
    patches_ref,
    coef_ref,
    kx_ref,
    ky_ref,
    coadd_ref,
    detect_ref,
    raw,
    tiles,
    down,
    across,
    mixed,
    mix_rows,
    bases,
    results,
    slot_piece,
    meta_send,
    meta_recv,
    x_send,
    x_recv,
    z_recv,
    stage,
    own_part,
    det_stage,
    load_sem,
    out_sem,
    meta_ssem,
    meta_rsem,
    x_ssem,
    x_rsem,
    z_ssem,
    z_rsem,
):
    pieces, side, taps, basis, sky, bands, cap, rows = sizes
    half = taps // 2
    me = lax.axis_index("sky")
    band = lax.axis_index("band")

    def sky_at(d):
        return lax.rem(me + d, sky)

    def band_at(d):
        return lax.rem(band + d, bands)

    barrier = pltpu.get_barrier_semaphore()
    for d in range(1, sky):
        pl.semaphore_signal(barrier, inc=1, device_id={"sky": sky_at(d)}, device_id_type=MESH)
    for d in range(1, bands):
        pl.semaphore_signal(barrier, inc=1, device_id={"band": band_at(d)}, device_id_type=MESH)

    loads = [
        pltpu.make_async_copy(patches_ref.at[s], raw.at[s], load_sem.at[s]) for s in range(pieces)
    ]
    for load in loads:
        load.start()

    owners = [owner_ref[s] for s in range(pieces)]
    ranks = []
    for s in range(pieces):
        rank = jnp.int32(0)
        for other in range(s):
            rank = rank + (owners[other] == owners[s]).astype(jnp.int32)
        ranks.append(owners[s] * cap + rank)
    weights = []
    for s in range(pieces):
        weight = jnp.full((1, 128), ivar_ref[visit_ref[s]], F32).astype(BF16).astype(F32)
        weights.append(weight)
        coefs = coef_ref[visit_ref[s]].astype(BF16).astype(F32)
        mix_rows[s : s + 1, :] = (coefs * weight[:, :1]).astype(BF16).astype(F32)
    for slot in range(sky * cap):
        piece = jnp.int32(0)
        used = jnp.int32(0)
        for s in range(pieces):
            hit = (ranks[s] == slot).astype(jnp.int32)
            piece = piece + hit * s
            used = used + hit
        slot_piece[slot] = piece
        dest, c = divmod(slot, cap)
        meta_send[dest, c : c + 1, :] = (
            jnp.full((1, 128), ivar_ref[visit_ref[piece]], F32).astype(BF16).astype(F32)
        )
        meta_send[dest, cap + c : cap + c + 1, :] = jnp.full(
            (1, 128), valid_ref[piece], jnp.int32
        ).astype(F32)
        meta_send[dest, 2 * cap + c : 2 * cap + c + 1, :] = jnp.full(
            (1, 128), local_ref[piece] * used + used - 1, jnp.int32
        ).astype(F32)
    meta_recv[me] = meta_send[me]

    wide = bases.shape[1]
    taps_at = lax.broadcasted_iota(jnp.int32, (taps, wide), 0) - half
    lanes = lax.broadcasted_iota(jnp.int32, (taps, wide), 1)
    for start, ref, away in ((0, ky_ref, taps_at), (basis, kx_ref, -taps_at)):
        place = (lanes == jnp.where(away < 0, away + wide, away)).astype(BF16)
        bases[start : start + basis, :] = jnp.dot(ref[...], place, preferred_element_type=F32)
    row_ids = lax.broadcasted_iota(jnp.int32, (side, side), 0)
    col_ids = lax.broadcasted_iota(jnp.int32, (side, side), 1)
    near = jnp.abs(row_ids - col_ids) <= half


    def table(k, start):
        row = jnp.broadcast_to(bases[pl.ds(start + k, 1), :], (wide, wide))
        ring = pltpu.roll(row, 0, 1, stride=1, stride_axis=0)
        many = side // wide
        full = jnp.concatenate([jnp.concatenate([ring] * many, axis=1)] * many, axis=0)
        return jnp.where(near, full, 0.0).astype(BF16)

    def make_tables(k, carry):
        one = table(k, 0)
        for chunk in range(bands):
            down[chunk, pl.ds(k * rows, rows), :] = one[chunk * rows : (chunk + 1) * rows]
        across[pl.ds(k * side, side), :] = table(k, basis)
        return carry

    lax.fori_loop(0, basis, make_tables, 0)

    for s in range(pieces):
        loads[s].wait()
        tiles[s] = jnp.where(row_ids < valid_ref[s], raw[s], 0.0).astype(BF16)

    pl.semaphore_wait(barrier, sky - 1 + bands - 1)

    def meta_copy(d):
        return pltpu.make_async_remote_copy(
            src_ref=meta_send.at[sky_at(d)],
            dst_ref=meta_recv.at[me],
            send_sem=meta_ssem.at[d],
            recv_sem=meta_rsem.at[d],
            device_id={"sky": sky_at(d)},
            device_id_type=MESH,
        )

    def sky_copy(t, d):
        return pltpu.make_async_remote_copy(
            src_ref=x_send.at[t, sky_at(d)],
            dst_ref=x_recv.at[t, me],
            send_sem=x_ssem.at[t, d],
            recv_sem=x_rsem.at[t, d],
            device_id={"sky": sky_at(d)},
            device_id_type=MESH,
        )

    offsets = band_offsets(bands)

    def band_copy(t):
        return pltpu.make_async_remote_copy(
            src_ref=stage.at[t],
            dst_ref=z_recv.at[t],
            send_sem=z_ssem.at[t],
            recv_sem=z_rsem.at[t],
            device_id={"band": band_at(offsets[t])},
            device_id_type=MESH,
        )

    def coadd_copy(t):
        chunk = band_at(offsets[t])
        return pltpu.make_async_copy(
            stage.at[t],
            coadd_ref.at[:, pl.ds(pl.multiple_of(chunk * rows, rows), rows), :],
            out_sem.at[t],
        )

    for d in range(1, sky):
        meta_copy(d).start()

    def convolve(t, early=None):
        chunk = band_at(offsets[t])

        def one_piece(s, carry):
            first = jnp.dot(down[chunk], tiles[s], preferred_element_type=F32)
            for k in range(basis):
                scale = jnp.broadcast_to(mix_rows[pl.ds(s, 1), k : k + 1], (rows, side))
                mixed[pl.ds(pl.multiple_of(s * rows, rows), rows), k * side : (k + 1) * side] = (
                    first[k * rows : (k + 1) * rows] * scale
                ).astype(BF16)
            return carry

        lax.fori_loop(0, pieces // 2, one_piece, 0)
        if early is not None:
            collect(early)
        lax.fori_loop(pieces // 2, pieces, one_piece, 0)
        done = jnp.dot(mixed[...], across[...], preferred_element_type=F32)
        results[...] = done.astype(BF16).reshape(pieces, rows, side)
        for d in range(1, sky):
            for c in range(cap):
                x_send[t, sky_at(d), c] = results[slot_piece[sky_at(d) * cap + c]]
        for d in range(1, sky):
            sky_copy(t, d).start()
        for c in range(cap):
            x_recv[t, me, c] = results[slot_piece[me * cap + c]]

    block = 16

    def collect(t):
        chunk = band_at(offsets[t])
        if t == 0:
            for d in range(1, sky):
                meta_copy(d).wait()
        for d in range(1, sky):
            sky_copy(t, d).wait_recv()

        def some_rows(r, carry):
            at = pl.multiple_of(r * block, block)
            line = lax.broadcasted_iota(jnp.int32, (block, 128), 0) + (chunk * rows + at)
            line = line.astype(F32)
            lane = lax.broadcasted_iota(jnp.int32, (block, 128), 1).astype(F32)
            cover = jnp.zeros((block, 128), F32)
            sums = [jnp.zeros((block, side), F32) for _ in range(PATCH_DEV)]
            for src in range(sky):
                for c in range(cap):
                    weight = meta_recv[src, c : c + 1, :]
                    count = meta_recv[src, cap + c : cap + c + 1, :]
                    local = meta_recv[src, 2 * cap + c : 2 * cap + c + 1, :]
                    cover = cover + jnp.where((lane == local) & (line < count), weight, 0.0)
                    local = jnp.broadcast_to(local[:, :1], (block, side))
                    piece = x_recv[t, src, c, pl.ds(at, block), :].astype(F32)
                    for p in range(PATCH_DEV):
                        sums[p] = sums[p] + jnp.where(local == float(p), piece, 0.0)
            scale = 1.0 / jnp.maximum(cover, 1.0)
            for p in range(PATCH_DEV):
                value = sums[p] * jnp.broadcast_to(scale[:, p : p + 1], (block, side))
                stage[t, p, pl.ds(at, block), :] = value.astype(BF16)
                if t == bands - 1:
                    own_part[p, pl.ds(at, block), :] = value
            return carry

        lax.fori_loop(0, rows // block, some_rows, 0)
        if t < bands - 1:
            band_copy(t).start()
        coadd_copy(t).start()

    convolve(0)
    for t in range(1, bands):
        convolve(t, t - 2 if t > 1 else None)
    if bands > 1:
        collect(bands - 2)
    collect(bands - 1)
    for t in range(bands - 1):
        band_copy(t).wait_recv()

    def add_bands(p, carry):
        total = own_part[p]
        for t in range(bands - 1):
            total = total + z_recv[t, p].astype(F32)
        det_stage[p] = total.astype(BF16)
        return carry

    lax.fori_loop(0, PATCH_DEV, add_bands, 0)
    last = pltpu.make_async_copy(det_stage, detect_ref, load_sem.at[0])
    last.start()
    for t in range(bands):
        for d in range(1, sky):
            sky_copy(t, d).wait_send()
        if t < bands - 1:
            band_copy(t).wait_send()
        coadd_copy(t).wait()
    last.wait()


def widen(coadd_in, detect_in, coadd_out, detect_out, coadd_a, detect_a, coadd_b, detect_b, in_sem, out_sem):
    pairs = ((coadd_in, coadd_a, coadd_b, coadd_out), (detect_in, detect_a, detect_b, detect_out))
    loads, stores = [], []
    for p in range(PATCH_DEV):
        for which, (source, narrow, wide, dest) in enumerate(pairs):
            loads.append(pltpu.make_async_copy(source.at[p], narrow.at[p], in_sem.at[which, p]))
            stores.append(pltpu.make_async_copy(wide.at[p], dest.at[p], out_sem.at[which, p]))
    for load in loads:
        load.start()
    for p in range(PATCH_DEV):
        for which, (source, narrow, wide, dest) in enumerate(pairs):
            loads[2 * p + which].wait()
            wide[p] = narrow[p].astype(F32)
            stores[2 * p + which].start()
    for store in stores:
        store.wait()


def per_device(
    patches, valid_rows, slot_owner, slot_local, slot_visit, basis_coef, inv_var, kernel_x, kernel_y
):
    pieces, side = patches.shape[1], patches.shape[2]
    basis, taps = kernel_x.shape
    sky, bands = lax.axis_size("sky"), lax.axis_size("band")
    cap = max(2, 2 * pieces // sky)
    rows = side // bands
    meta_rows = -(-3 * cap // 8) * 8
    smem = pl.BlockSpec(memory_space=pltpu.SMEM)
    vmem = pl.BlockSpec(memory_space=pltpu.VMEM)
    hbm = pl.BlockSpec(memory_space=pl.ANY)
    sizes = (pieces, side, taps, basis, sky, bands, cap, rows)
    coadd, detection = pl.pallas_call(
        functools.partial(kernel, sizes),
        out_shape=(
            jax.ShapeDtypeStruct((PATCH_DEV, side, side), BF16),
            jax.ShapeDtypeStruct((PATCH_DEV, rows, side), BF16),
        ),
        in_specs=[smem] * 5 + [hbm, vmem, vmem, vmem],
        out_specs=(hbm, hbm),
        scratch_shapes=[
            pltpu.VMEM((pieces, side, side), F32),
            pltpu.VMEM((pieces, side, side), BF16),
            pltpu.VMEM((bands, basis * rows, side), BF16),
            pltpu.VMEM((basis * side, side), BF16),
            pltpu.VMEM((pieces * rows, basis * side), BF16),
            pltpu.VMEM((pieces, basis), F32),
            pltpu.VMEM((2 * basis, 128), F32),
            pltpu.VMEM((pieces, rows, side), BF16),
            pltpu.SMEM((sky * cap,), jnp.int32),
            pltpu.VMEM((sky, meta_rows, 128), F32),
            pltpu.VMEM((sky, meta_rows, 128), F32),
            pltpu.VMEM((bands, sky, cap, rows, side), BF16),
            pltpu.VMEM((bands, sky, cap, rows, side), BF16),
            pltpu.VMEM((max(1, bands - 1), PATCH_DEV, rows, side), BF16),
            pltpu.VMEM((bands, PATCH_DEV, rows, side), BF16),
            pltpu.VMEM((PATCH_DEV, rows, side), F32),
            pltpu.VMEM((PATCH_DEV, rows, side), BF16),
            pltpu.SemaphoreType.DMA((pieces,)),
            pltpu.SemaphoreType.DMA((bands,)),
            pltpu.SemaphoreType.DMA((sky,)),
            pltpu.SemaphoreType.DMA((sky,)),
            pltpu.SemaphoreType.DMA((bands, sky)),
            pltpu.SemaphoreType.DMA((bands, sky)),
            pltpu.SemaphoreType.DMA((bands,)),
            pltpu.SemaphoreType.DMA((bands,)),
        ],
        compiler_params=pltpu.CompilerParams(
            collective_id=0, has_side_effects=True, vmem_limit_bytes=60 * 1024 * 1024
        ),
    )(
        valid_rows[0],
        slot_owner[0, :, 0],
        slot_local[0],
        slot_visit[0],
        inv_var[0],
        patches[0],
        jnp.transpose(basis_coef, (1, 0, 2)),
        kernel_x,
        kernel_y,
    )
    coadd, detection = pl.pallas_call(
        widen,
        out_shape=(
            jax.ShapeDtypeStruct(coadd.shape, F32),
            jax.ShapeDtypeStruct(detection.shape, F32),
        ),
        in_specs=[hbm, hbm],
        out_specs=(hbm, hbm),
        scratch_shapes=[
            pltpu.VMEM(coadd.shape, BF16),
            pltpu.VMEM(detection.shape, BF16),
            pltpu.VMEM(coadd.shape, F32),
            pltpu.VMEM(detection.shape, F32),
            pltpu.SemaphoreType.DMA((2, PATCH_DEV)),
            pltpu.SemaphoreType.DMA((2, PATCH_DEV)),
        ],
    )(coadd, detection)
    return coadd[None], detection


def solution(mesh):
    in_specs = (
        P(("tract", "band"), "sky", None, None),
        P(("tract", "band"), "sky"),
        P(("tract", "band"), "sky", None),
        P(("tract", "band"), "sky"),
        P(("tract", "band"), "sky"),
        P(("tract", "band"), None, None),
        P(("tract", "band"), None),
        P(),
        P(),
    )
    out_specs = (P(("tract", "band"), "sky", None, None), P(("tract", "sky"), "band", None))
    return jax.shard_map(
        per_device, mesh=mesh, in_specs=in_specs, out_specs=out_specs, check_vma=False
    )
```

profile of v0, /device:TPU:0, one launch (start us, length us, event | category | flops | bytes accessed | tf_op | source)
XLA Modules:
  0.0 47.6 jit_solution(14076324231526662362)
XLA Ops:
  0.6 44.3 %shard_map.104 = (bf16[8,256,256]{2,1,0:T(8,128)(2,1)}, bf16[8,64,256]{2,1,0:T(8,128)(2,1)}) custom-call(s32[8]{0:T(128)} %bitcast.10, s32[8]{0:T(128)} %bitcast.11, s32[8]{0:T(128)} %bitcast.12, s32[8]{0:T(128)} %bitcast.13, f32[12]{0:T(128)} %bitcast.14, f32[8,256,256]{2,1,0:T(8,128)} %bitcast.8, f32[12,1,21]{2,1,0:T(1,128)} %bitcast.9, ...), custom_call_target="tpu_custom_call" | custom-call | tf_op jit(solution)/shard_map/pallas_call | solution.py:317
  45.0 2.7 %shard_map.105 = (f32[8,256,256]{2,1,0:T(8,128)}, f32[8,64,256]{2,1,0:T(8,128)}) custom-call(bf16[8,256,256]{2,1,0:T(8,128)(2,1)} %get-tuple-element.6.coadd_in, bf16[8,64,256]{2,1,0:T(8,128)(2,1)} %get-tuple-element.7.detect_in), custom_call_target="tpu_custom_call" | custom-call | tf_op jit(solution)/shard_map/pallas_call | solution.py:366
where the time goes:
time: 47.8 us; the launch traced here: 47.6 us
  Pallas kernels  47 us (98%)
  between operations  0.64 us (1%)
    pallas_call x1, Pallas kernels, per_device(): pl.pallas_call(functools.partial(kernel, sizes), out_shape=(jax.ShapeDtyp...  44.3 us
    pallas_call x1, Pallas kernels, per_device(): pl.pallas_call(widen, out_shape=(jax.ShapeDtypeStruct(coadd.shape, F32),...  2.67 us

commit v1 on v0

v1 whole, which is shorter than its diff:
```python
import functools

import jax
import jax.numpy as jnp
from jax import lax
from jax.experimental import pallas as pl
from jax.experimental.pallas import tpu as pltpu
from jax.sharding import PartitionSpec as P

PATCH_DEV = 8
MESH = pl.DeviceIdType.MESH
F32 = jnp.float32
BF16 = jnp.bfloat16


def chunk_at(t, bands, subs):
    if bands == 1:
        return t * 0, t
    far = (bands - 2) * subs
    near = lax.div(t, far) if far else t * 0 + 1
    pair = lax.rem(t, 2 * subs)
    last = t - far
    offset = (1 - near) * (bands - 1 - 2 * lax.div(t, 2 * subs) - lax.rem(pair, 2))
    offset = offset + near * (1 - lax.div(last, subs))
    return offset, (1 - near) * lax.div(pair, 2) + near * lax.rem(last, subs)


def flip(index, bits, top):
    result = index
    for i in range((top - 1).bit_length()):
        bit = lax.rem(lax.div(bits, 1 << i), 2)
        result = result + (1 << i) * bit * (1 - 2 * lax.rem(lax.div(index, 1 << i), 2))
    return result


def kernel(
    sizes,
    valid_ref,
    owner_ref,
    local_ref,
    visit_ref,
    ivar_ref,
    patches_ref,
    coef_ref,
    kx_ref,
    ky_ref,
    coadd_ref,
    detect_ref,
    raw,
    tiles,
    down,
    across,
    mixed,
    mixing,
    bases,
    results,
    slot_piece,
    meta_send,
    meta_recv,
    x_send,
    x_recv,
    z_recv,
    stage,
    values,
    final,
    det_stage,
    load_sem,
    out_sem,
    det_sem,
    meta_ssem,
    meta_rsem,
    x_ssem,
    x_rsem,
    z_ssem,
    z_rsem,
):
    pieces, side, taps, basis, sky, bands, cap, rows, part, pad = sizes
    half = taps // 2
    window = part + 2 * pad
    me = lax.axis_index("sky")
    band = lax.axis_index("band")
    subs = rows // part
    chunks = bands * subs
    evens = list(range(2, bands, 2))

    def chunk_of(t):
        return chunk_at(jnp.int32(t), bands, subs)

    def band_at(r):
        return flip(band, jnp.int32(r), bands)

    def sky_at(d):
        return lax.rem(me + d, sky)

    barrier = pltpu.get_barrier_semaphore()
    for d in range(1, sky):
        pl.semaphore_signal(barrier, inc=1, device_id={"sky": sky_at(d)}, device_id_type=MESH)
    band_peers = ([1] if bands > 1 else []) + evens
    for r in band_peers:
        pl.semaphore_signal(barrier, inc=1, device_id={"band": band_at(r)}, device_id_type=MESH)

    loads = [
        pltpu.make_async_copy(patches_ref.at[s], raw.at[s], load_sem.at[s]) for s in range(pieces)
    ]
    for load in loads:
        load.start()

    owners = [owner_ref[s] for s in range(pieces)]
    ranks = []
    for s in range(pieces):
        rank = jnp.int32(0)
        for other in range(s):
            rank = rank + (owners[other] == owners[s]).astype(jnp.int32)
        ranks.append(owners[s] * cap + rank)
    tall = -(-basis // 8) * 8
    on_lane = lax.broadcasted_iota(jnp.int32, (tall, basis), 1)
    on_row = lax.broadcasted_iota(jnp.int32, (tall, basis), 0)
    for s in range(pieces):
        weight = jnp.full((1, basis), ivar_ref[visit_ref[s]], F32).astype(BF16).astype(F32)
        coefs = coef_ref[visit_ref[s]].astype(BF16).astype(F32)
        mix = (coefs * weight).astype(BF16).astype(F32)
        column = jnp.sum(
            jnp.where(on_lane == on_row, jnp.broadcast_to(mix, (tall, basis)), 0.0),
            axis=1,
            keepdims=True,
        )
        mixing[s] = jnp.broadcast_to(column, (tall, side))
    for slot in range(sky * cap):
        piece = jnp.int32(0)
        used = jnp.int32(0)
        for s in range(pieces):
            hit = (ranks[s] == slot).astype(jnp.int32)
            piece = piece + hit * s
            used = used + hit
        slot_piece[slot] = piece
        dest, c = divmod(slot, cap)
        meta_send[dest, c : c + 1, :] = (
            jnp.full((1, 128), ivar_ref[visit_ref[piece]], F32).astype(BF16).astype(F32)
        )
        meta_send[dest, cap + c : cap + c + 1, :] = jnp.full(
            (1, 128), valid_ref[piece], jnp.int32
        ).astype(F32)
        meta_send[dest, 2 * cap + c : 2 * cap + c + 1, :] = jnp.full(
            (1, 128), local_ref[piece] * used + used - 1, jnp.int32
        ).astype(F32)
    meta_recv[me] = meta_send[me]

    wide = bases.shape[1]
    taps_at = lax.broadcasted_iota(jnp.int32, (taps, wide), 0) - half
    lanes = lax.broadcasted_iota(jnp.int32, (taps, wide), 1)
    for start, ref, away in ((0, ky_ref, pad + taps_at), (basis, kx_ref, -taps_at)):
        place = (lanes == jnp.where(away < 0, away + wide, away)).astype(BF16)
        bases[start : start + basis, :] = jnp.dot(ref[...], place, preferred_element_type=F32)
    ring_row = lax.broadcasted_iota(jnp.int32, (wide, wide), 0)
    ring_col = lax.broadcasted_iota(jnp.int32, (wide, wide), 1)
    blocks = side // wide

    def make_tables(k, carry):
        row = jnp.broadcast_to(bases[pl.ds(k, 1), :], (part, wide))
        shifted = pltpu.roll(row, 0, 1, stride=1, stride_axis=0)
        down[pl.ds(pl.multiple_of(k * part, part), part), :] = shifted[:, :window].astype(BF16)
        row = jnp.broadcast_to(bases[pl.ds(basis + k, 1), :], (wide, wide))
        ring = pltpu.roll(row, 0, 1, stride=1, stride_axis=0)
        on = jnp.where(jnp.abs(ring_row - ring_col) <= half, ring, 0.0).astype(BF16)
        below = jnp.where(ring_col - ring_row >= wide - half, ring, 0.0).astype(BF16)
        above = jnp.where(ring_row - ring_col >= wide - half, ring, 0.0).astype(BF16)
        none = jnp.zeros((wide, wide), BF16)
        pick = {0: on, 1: below, -1: above}
        for i in range(blocks):
            for j in range(blocks):
                spot = pl.ds(pl.multiple_of(k * side + i * wide, wide), wide)
                across[spot, j * wide : (j + 1) * wide] = pick.get(i - j, none)
        return carry

    lax.fori_loop(0, basis, make_tables, 0)

    row_ids = lax.broadcasted_iota(jnp.int32, (side, side), 0)
    for s in range(pieces):
        tiles[s, 0:pad, :] = jnp.zeros((pad, side), BF16)
        tiles[s, pad + side : side + 2 * pad, :] = jnp.zeros((pad, side), BF16)
        loads[s].wait()
        tiles[s, pad : pad + side, :] = jnp.where(row_ids < valid_ref[s], raw[s], 0.0).astype(BF16)

    def meta_copy(d):
        return pltpu.make_async_remote_copy(
            src_ref=meta_send.at[sky_at(d)],
            dst_ref=meta_recv.at[me],
            send_sem=meta_ssem.at[d],
            recv_sem=meta_rsem.at[d],
            device_id={"sky": sky_at(d)},
            device_id_type=MESH,
        )

    def sky_copy(t, d):
        return pltpu.make_async_remote_copy(
            src_ref=x_send.at[t, sky_at(d)],
            dst_ref=x_recv.at[t, me],
            send_sem=x_ssem.at[t, d],
            recv_sem=x_rsem.at[t, d],
            device_id={"sky": sky_at(d)},
            device_id_type=MESH,
        )

    def band_copy(t, r, source):
        return pltpu.make_async_remote_copy(
            src_ref=source.at[t],
            dst_ref=z_recv.at[t],
            send_sem=z_ssem.at[t],
            recv_sem=z_rsem.at[t],
            device_id={"band": band_at(r)},
            device_id_type=MESH,
        )

    def first_row(t):
        r, sub = chunk_of(t)
        return pl.multiple_of(band_at(r) * rows + sub * part, part)

    def coadd_copy(t):
        return pltpu.make_async_copy(
            final.at[t], coadd_ref.at[:, pl.ds(first_row(t), part), :], out_sem.at[t]
        )

    def detect_copy(sub):
        return pltpu.make_async_copy(
            det_stage.at[sub], detect_ref.at[:, pl.ds(pl.multiple_of(sub * part, part), part), :], det_sem.at[sub]
        )

    def convolve(t):
        rows_in = pl.ds(first_row(t), window)
        for s in range(pieces):
            first = jnp.dot(down[...], tiles[s, rows_in, :], preferred_element_type=F32)
            for k in range(basis):
                scale = jnp.broadcast_to(mixing[s, k : k + 1, :], (part, side))
                mixed[s * part : (s + 1) * part, k * side : (k + 1) * side] = (
                    first[k * part : (k + 1) * part] * scale
                ).astype(BF16)

        def second(_, carry):
            done = jnp.dot(mixed[...], across[...], preferred_element_type=F32)
            results[...] = done.astype(BF16).reshape(pieces, part, side)
            return carry

        once = lax.div(t, chunks) + 1
        lax.fori_loop(0, once, second, 0)

        def to_slots(_, carry):
            for slot in range(sky * cap):
                x_send[t, slot // cap, slot % cap] = results[slot_piece[slot]]
            for c in range(cap):
                x_recv[t, me, c] = results[slot_piece[me * cap + c]]
            return carry

        lax.fori_loop(0, once, to_slots, 0)

        @pl.when(t == 0)
        def _():
            pl.semaphore_wait(barrier, sky - 1 + len(band_peers))
            for d in range(1, sky):
                meta_copy(d).start()

        for d in range(1, sky):
            sky_copy(t, d).start()

    block = 16
    late = lax.rem(me, 2) == 1

    def collect(t):
        r, sub = chunk_of(t)

        @pl.when(t == 0)
        def _():
            for d in range(1, sky):
                meta_copy(d).wait()

        for d in range(1, sky):
            sky_copy(t, d).wait_recv()
        base = first_row(t)

        def some_rows(i, carry):
            spot = pl.ds(pl.multiple_of(i * block, block), block)
            line = lax.broadcasted_iota(jnp.int32, (block, 128), 0) + (base + i * block)
            line = line.astype(F32)
            lane = lax.broadcasted_iota(jnp.int32, (block, 128), 1).astype(F32)
            cover = jnp.zeros((block, 128), F32)
            sums = [jnp.zeros((block, side), F32) for _ in range(PATCH_DEV)]
            for src in range(sky):
                for c in range(cap):
                    weight = meta_recv[src, c : c + 1, :]
                    count = meta_recv[src, cap + c : cap + c + 1, :]
                    local = meta_recv[src, 2 * cap + c : 2 * cap + c + 1, :]
                    cover = cover + jnp.where((lane == local) & (line < count), weight, 0.0)
                    local = jnp.broadcast_to(local[:, :1], (block, side))
                    piece = x_recv[t, src, c, spot, :].astype(F32)
                    for p in range(PATCH_DEV):
                        sums[p] = sums[p] + jnp.where(local == float(p), piece, 0.0)
            scale = 1.0 / jnp.maximum(cover, 1.0)
            for p in range(PATCH_DEV):
                value = sums[p] * jnp.broadcast_to(scale[:, p : p + 1], (block, side))
                final[t, p, spot, :] = value.astype(BF16)
                values[p, spot, :] = value
            return carry

        lax.fori_loop(0, part // block, some_rows, 0)
        coadd_copy(t).start()

        @pl.when(lax.rem(r, 2) == 1)
        def _():
            band_copy(t, 1, final).start()

            @pl.when(late & (t > 0))
            def _():
                before = chunk_of(t - 1)[0]

                @pl.when(lax.rem(before, 2) == 0)
                def _():
                    band_copy(t - 1, before, stage).start()

        @pl.when((lax.rem(r, 2) == 0) & (r > 0))
        def _():
            band_copy(t - 1, 1, final).wait_recv()

            def add(p, carry):
                stage[t, p] = (values[p] + z_recv[t - 1, p].astype(F32)).astype(BF16)
                return carry

            lax.fori_loop(0, PATCH_DEV, add, 0)

            @pl.when(jnp.logical_not(late))
            def _():
                band_copy(t, r, stage).start()

        @pl.when(r == 0)
        def _():
            others = [t - subs] if bands > 1 else []
            for q in evens:
                others.append((bands - 2 - q) * subs + 2 * sub + 1)
            for other in others:
                band_copy(other, 1, final).wait_recv()

            def add(p, carry):
                total = values[p]
                for other in others:
                    total = total + z_recv[other, p].astype(F32)
                det_stage[sub, p] = total.astype(BF16)
                return carry

            lax.fori_loop(0, PATCH_DEV, add, 0)
            detect_copy(sub).start()

    lag = 2

    def step(t, carry):
        @pl.when(t < chunks)
        def _():
            convolve(t)

        @pl.when(t >= lag)
        def _():
            collect(t - lag)

        return carry

    lax.fori_loop(0, chunks + lag, step, 0)

    def finish(t, carry):
        r, sub = chunk_of(t)
        for d in range(1, sky):
            sky_copy(t, d).wait_send()
        coadd_copy(t).wait()

        @pl.when(r > 0)
        def _():
            band_copy(t, 1, final).wait_send()

        @pl.when(r == 0)
        def _():
            detect_copy(sub).wait()

        return carry

    lax.fori_loop(0, chunks, finish, 0)


def widen(coadd_in, detect_in, coadd_out, detect_out, coadd_a, detect_a, coadd_b, detect_b, in_sem, out_sem):
    pairs = ((coadd_in, coadd_a, coadd_b, coadd_out), (detect_in, detect_a, detect_b, detect_out))
    loads, stores = [], []
    for p in range(PATCH_DEV):
        for which, (source, narrow, wide, dest) in enumerate(pairs):
            loads.append(pltpu.make_async_copy(source.at[p], narrow.at[p], in_sem.at[which, p]))
            stores.append(pltpu.make_async_copy(wide.at[p], dest.at[p], out_sem.at[which, p]))
    for load in loads:
        load.start()
    for p in range(PATCH_DEV):
        for which, (source, narrow, wide, dest) in enumerate(pairs):
            loads[2 * p + which].wait()
            wide[p] = narrow[p].astype(F32)
            stores[2 * p + which].start()
    for store in stores:
        store.wait()


def per_device(
    patches, valid_rows, slot_owner, slot_local, slot_visit, basis_coef, inv_var, kernel_x, kernel_y
):
    pieces, side = patches.shape[1], patches.shape[2]
    basis, taps = kernel_x.shape
    sky, bands = lax.axis_size("sky"), lax.axis_size("band")
    cap = max(2, 2 * pieces // sky)
    rows = side // bands
    part = min(rows, 32)
    pad = -(-(taps // 2) // 16) * 16
    chunks = side // part
    meta_rows = -(-3 * cap // 8) * 8
    smem = pl.BlockSpec(memory_space=pltpu.SMEM)
    vmem = pl.BlockSpec(memory_space=pltpu.VMEM)
    hbm = pl.BlockSpec(memory_space=pl.ANY)
    sizes = (pieces, side, taps, basis, sky, bands, cap, rows, part, pad)
    coadd, detection = pl.pallas_call(
        functools.partial(kernel, sizes),
        out_shape=(
            jax.ShapeDtypeStruct((PATCH_DEV, side, side), BF16),
            jax.ShapeDtypeStruct((PATCH_DEV, rows, side), BF16),
        ),
        in_specs=[smem] * 5 + [hbm, vmem, vmem, vmem],
        out_specs=(hbm, hbm),
        scratch_shapes=[
            pltpu.VMEM((pieces, side, side), F32),
            pltpu.VMEM((pieces, side + 2 * pad, side), BF16),
            pltpu.VMEM((basis * part, part + 2 * pad), BF16),
            pltpu.VMEM((basis * side, side), BF16),
            pltpu.VMEM((pieces * part, basis * side), BF16),
            pltpu.VMEM((pieces, -(-basis // 8) * 8, side), F32),
            pltpu.VMEM((2 * basis, 128), F32),
            pltpu.VMEM((pieces, part, side), BF16),
            pltpu.SMEM((sky * cap,), jnp.int32),
            pltpu.VMEM((sky, meta_rows, 128), F32),
            pltpu.VMEM((sky, meta_rows, 128), F32),
            pltpu.VMEM((chunks, sky, cap, part, side), BF16),
            pltpu.VMEM((chunks, sky, cap, part, side), BF16),
            pltpu.VMEM((chunks, PATCH_DEV, part, side), BF16),
            pltpu.VMEM((chunks, PATCH_DEV, part, side), BF16),
            pltpu.VMEM((PATCH_DEV, part, side), F32),
            pltpu.VMEM((chunks, PATCH_DEV, part, side), BF16),
            pltpu.VMEM((rows // part, PATCH_DEV, part, side), BF16),
            pltpu.SemaphoreType.DMA((pieces,)),
            pltpu.SemaphoreType.DMA((chunks,)),
            pltpu.SemaphoreType.DMA((rows // part,)),
            pltpu.SemaphoreType.DMA((sky,)),
            pltpu.SemaphoreType.DMA((sky,)),
            pltpu.SemaphoreType.DMA((chunks, sky)),
            pltpu.SemaphoreType.DMA((chunks, sky)),
            pltpu.SemaphoreType.DMA((chunks,)),
            pltpu.SemaphoreType.DMA((chunks,)),
        ],
        compiler_params=pltpu.CompilerParams(
            collective_id=0, has_side_effects=True, vmem_limit_bytes=60 * 1024 * 1024
        ),
    )(
        valid_rows[0],
        slot_owner[0, :, 0],
        slot_local[0],
        slot_visit[0],
        inv_var[0],
        patches[0],
        jnp.transpose(basis_coef, (1, 0, 2)),
        kernel_x,
        kernel_y,
    )
    coadd, detection = pl.pallas_call(
        widen,
        out_shape=(
            jax.ShapeDtypeStruct(coadd.shape, F32),
            jax.ShapeDtypeStruct(detection.shape, F32),
        ),
        in_specs=[hbm, hbm],
        out_specs=(hbm, hbm),
        scratch_shapes=[
            pltpu.VMEM(coadd.shape, BF16),
            pltpu.VMEM(detection.shape, BF16),
            pltpu.VMEM(coadd.shape, F32),
            pltpu.VMEM(detection.shape, F32),
            pltpu.SemaphoreType.DMA((2, PATCH_DEV)),
            pltpu.SemaphoreType.DMA((2, PATCH_DEV)),
        ],
    )(coadd, detection)
    return coadd[None], detection


def solution(mesh):
    in_specs = (
        P(("tract", "band"), "sky", None, None),
        P(("tract", "band"), "sky"),
        P(("tract", "band"), "sky", None),
        P(("tract", "band"), "sky"),
        P(("tract", "band"), "sky"),
        P(("tract", "band"), None, None),
        P(("tract", "band"), None),
        P(),
        P(),
    )
    out_specs = (P(("tract", "band"), "sky", None, None), P(("tract", "sky"), "band", None))
    return jax.shard_map(
        per_device, mesh=mesh, in_specs=in_specs, out_specs=out_specs, check_vma=False
    )
```

time: 47.8 us -> 42.3 us (0.88)
  Pallas kernels: 47 us -> 41.5 us
    pallas_call x1, Pallas kernels: 44.3 us -> 38.8 us  [per_device(): pl.pallas_call(functools.partial(kernel, sizes), out_shape=(jax.ShapeDtyp...]
where the time goes in v1:
time: 42.3 us; the launch traced here: 42.1 us
  Pallas kernels  41.5 us (98%)
  between operations  0.64 us (2%)
    pallas_call x1, Pallas kernels, per_device(): pl.pallas_call(functools.partial(kernel, sizes), out_shape=(jax.ShapeDtyp...  38.8 us
    pallas_call x1, Pallas kernels, per_device(): pl.pallas_call(widen, out_shape=(jax.ShapeDtypeStruct(coadd.shape, F32),...  2.67 us

profile of v1, /device:TPU:0, one launch (start us, length us, event | category | flops | bytes accessed | tf_op | source)
XLA Modules:
  0.0 42.1 jit_solution(18241342207014560399)
XLA Ops:
  0.6 38.8 %shard_map.104 = (bf16[8,256,256]{2,1,0:T(8,128)(2,1)}, bf16[8,64,256]{2,1,0:T(8,128)(2,1)}) custom-call(s32[8]{0:T(128)} %bitcast.10, s32[8]{0:T(128)} %bitcast.11, s32[8]{0:T(128)} %bitcast.12, s32[8]{0:T(128)} %bitcast.13, f32[12]{0:T(128)} %bitcast.14, f32[8,256,256]{2,1,0:T(8,128)} %bitcast.8, f32[12,1,21]{2,1,0:T(1,128)} %bitcast.9, ...), custom_call_target="tpu_custom_call" | custom-call | tf_op jit(solution)/shard_map/pallas_call | solution.py:418
  39.4 2.7 %shard_map.105 = (f32[8,256,256]{2,1,0:T(8,128)}, f32[8,64,256]{2,1,0:T(8,128)}) custom-call(bf16[8,256,256]{2,1,0:T(8,128)(2,1)} %get-tuple-element.6.coadd_in, bf16[8,64,256]{2,1,0:T(8,128)(2,1)} %get-tuple-element.7.detect_in), custom_call_target="tpu_custom_call" | custom-call | tf_op jit(solution)/shard_map/pallas_call | solution.py:469

commit v2 on v1

--- a/solution.py
+++ b/solution.py
@@ -95,9 +95,28 @@
     barrier = pltpu.get_barrier_semaphore()
     for d in range(1, sky):
         pl.semaphore_signal(barrier, inc=1, device_id={"sky": sky_at(d)}, device_id_type=MESH)
-    band_peers = ([1] if bands > 1 else []) + evens
-    for r in band_peers:
-        pl.semaphore_signal(barrier, inc=1, device_id={"band": band_at(r)}, device_id_type=MESH)
+    odd = lax.rem(band, 2)
+
+    def up(r):
+        return lax.div(band_at(r) - band - 1 + bands, bands)
+
+    def outer(r):
+        return up(r) * (1 - odd) + (1 - up(r)) * odd
+
+    greeted = jnp.int32(sky - 1)
+    for r in range(1, bands):
+
+        def greet(r=r):
+            pl.semaphore_signal(
+                barrier, inc=1, device_id={"band": band_at(r)}, device_id_type=MESH
+            )
+
+        if r % 2 and r > 1:
+            pl.when(outer(r) == 0)(greet)
+            greeted = greeted + 1 - outer(r)
+        else:
+            greet()
+            greeted = greeted + 1
 
     loads = [
         pltpu.make_async_copy(patches_ref.at[s], raw.at[s], load_sem.at[s]) for s in range(pieces)
@@ -201,12 +220,12 @@
             device_id_type=MESH,
         )
 
-    def band_copy(t, r, source):
+    def band_copy(t, r, source, hop):
         return pltpu.make_async_remote_copy(
             src_ref=source.at[t],
-            dst_ref=z_recv.at[t],
+            dst_ref=z_recv.at[hop, t],
             send_sem=z_ssem.at[t],
-            recv_sem=z_rsem.at[t],
+            recv_sem=z_rsem.at[hop, t],
             device_id={"band": band_at(r)},
             device_id_type=MESH,
         )
@@ -254,7 +273,7 @@
 
         @pl.when(t == 0)
         def _():
-            pl.semaphore_wait(barrier, sky - 1 + len(band_peers))
+            pl.semaphore_wait(barrier, greeted)
             for d in range(1, sky):
                 meta_copy(d).start()
 
@@ -262,8 +281,6 @@
             sky_copy(t, d).start()
 
     block = 16
-    late = lax.rem(me, 2) == 1
-
     def collect(t):
         r, sub = chunk_of(t)
 
@@ -297,56 +314,64 @@
             for p in range(PATCH_DEV):
                 value = sums[p] * jnp.broadcast_to(scale[:, p : p + 1], (block, side))
                 final[t, p, spot, :] = value.astype(BF16)
-                values[p, spot, :] = value
+                values[lax.rem(t, 4), p, spot, :] = value
             return carry
 
         lax.fori_loop(0, part // block, some_rows, 0)
         coadd_copy(t).start()
 
-        @pl.when(lax.rem(r, 2) == 1)
-        def _():
-            band_copy(t, 1, final).start()
-
-            @pl.when(late & (t > 0))
-            def _():
-                before = chunk_of(t - 1)[0]
-
-                @pl.when(lax.rem(before, 2) == 0)
-                def _():
-                    band_copy(t - 1, before, stage).start()
-
-        @pl.when((lax.rem(r, 2) == 0) & (r > 0))
-        def _():
-            band_copy(t - 1, 1, final).wait_recv()
+        @pl.when((r == 1) | ((r > 1) & (outer(r) == 1)))
+        def _():
+            band_copy(t, 1, final, 0).start()
+
+        @pl.when(r == 0)
+        def _():
+            others = [(0, t - subs)] if bands > 1 else []
+            for q in evens:
+                through = up(q) * odd + (1 - up(q)) * (1 - odd)
+                others.append((1, (bands - 2 - q) * subs + 2 * sub + 1 - through))
+            for hop, other in others:
+                band_copy(other, 1, final, hop).wait_recv()
 
             def add(p, carry):
-                stage[t, p] = (values[p] + z_recv[t - 1, p].astype(F32)).astype(BF16)
-                return carry
-
-            lax.fori_loop(0, PATCH_DEV, add, 0)
-
-            @pl.when(jnp.logical_not(late))
-            def _():
-                band_copy(t, r, stage).start()
-
-        @pl.when(r == 0)
-        def _():
-            others = [t - subs] if bands > 1 else []
-            for q in evens:
-                others.append((bands - 2 - q) * subs + 2 * sub + 1)
-            for other in others:
-                band_copy(other, 1, final).wait_recv()
-
-            def add(p, carry):
-                total = values[p]
-                for other in others:
-                    total = total + z_recv[other, p].astype(F32)
+                total = values[lax.rem(t, 4), p]
+                for hop, other in others:
+                    total = total + z_recv[hop, other, p].astype(F32)
                 det_stage[sub, p] = total.astype(BF16)
                 return carry
 
             lax.fori_loop(0, PATCH_DEV, add, 0)
             detect_copy(sub).start()
 
+    def forward(t, other):
+        r = chunk_of(t)[0]
+
+        @pl.when(outer(r) == 0)
+        def _():
+            band_copy(other, 1, final, 0).wait_recv()
+
+            def add(p, carry):
+                near = values[lax.rem(t, 4), p]
+                stage[t, p] = (near + z_recv[0, other, p].astype(F32)).astype(BF16)
+                return carry
+
+            lax.fori_loop(0, PATCH_DEV, add, 0)
+            band_copy(t, r, stage, 1).start()
+
+    far = (bands - 2) * subs
+
+    def forwards(t):
+        if far <= 0:
+            return
+
+        @pl.when((lax.rem(t, 2) == 0) & (t >= 2) & (t <= far))
+        def _():
+            forward(t - 1, t - 2)
+
+        @pl.when((lax.rem(t, 2) == 1) & (t >= 3) & (t <= far + 1))
+        def _():
+            forward(t - 3, t - 2)
+
     lag = 2
 
     def step(t, carry):
@@ -357,6 +382,7 @@
         @pl.when(t >= lag)
         def _():
             collect(t - lag)
+            forwards(t - lag)
 
         return carry
 
@@ -370,7 +396,7 @@
 
         @pl.when(r > 0)
         def _():
-            band_copy(t, 1, final).wait_send()
+            band_copy(t, 1, final, 0).wait_send()
 
         @pl.when(r == 0)
         def _():
@@ -437,9 +463,9 @@
             pltpu.VMEM((sky, meta_rows, 128), F32),
             pltpu.VMEM((chunks, sky, cap, part, side), BF16),
             pltpu.VMEM((chunks, sky, cap, part, side), BF16),
+            pltpu.VMEM((2, chunks, PATCH_DEV, part, side), BF16),
             pltpu.VMEM((chunks, PATCH_DEV, part, side), BF16),
-            pltpu.VMEM((chunks, PATCH_DEV, part, side), BF16),
-            pltpu.VMEM((PATCH_DEV, part, side), F32),
+            pltpu.VMEM((4, PATCH_DEV, part, side), F32),
             pltpu.VMEM((chunks, PATCH_DEV, part, side), BF16),
             pltpu.VMEM((rows // part, PATCH_DEV, part, side), BF16),
             pltpu.SemaphoreType.DMA((pieces,)),
@@ -450,7 +476,7 @@
             pltpu.SemaphoreType.DMA((chunks, sky)),
             pltpu.SemaphoreType.DMA((chunks, sky)),
             pltpu.SemaphoreType.DMA((chunks,)),
-            pltpu.SemaphoreType.DMA((chunks,)),
+            pltpu.SemaphoreType.DMA((2, chunks)),
         ],
         compiler_params=pltpu.CompilerParams(
             collective_id=0, has_side_effects=True, vmem_limit_bytes=60 * 1024 * 1024

time: 42.3 us -> 39.4 us (0.931)
  Pallas kernels: 41.5 us -> 38.4 us
    pallas_call x1, Pallas kernels: 38.8 us -> 35.7 us  [per_device(): pl.pallas_call(functools.partial(kernel, sizes), out_shape=(jax.ShapeDtyp...]
where the time goes in v2:
time: 39.4 us; the launch traced here: 39 us
  Pallas kernels  38.4 us (97%)
  between operations  0.64 us (2%)
    pallas_call x1, Pallas kernels, per_device(): pl.pallas_call(functools.partial(kernel, sizes), out_shape=(jax.ShapeDtyp...  35.7 us
    pallas_call x1, Pallas kernels, per_device(): pl.pallas_call(widen, out_shape=(jax.ShapeDtypeStruct(coadd.shape, F32),...  2.67 us

profile of v2, /device:TPU:0, one launch (start us, length us, event | category | flops | bytes accessed | tf_op | source)
XLA Modules:
  0.0 39.0 jit_solution(12089632893326463062)
XLA Ops:
  0.6 35.7 %shard_map.104 = (bf16[8,256,256]{2,1,0:T(8,128)(2,1)}, bf16[8,64,256]{2,1,0:T(8,128)(2,1)}) custom-call(s32[8]{0:T(128)} %bitcast.10, s32[8]{0:T(128)} %bitcast.11, s32[8]{0:T(128)} %bitcast.12, s32[8]{0:T(128)} %bitcast.13, f32[12]{0:T(128)} %bitcast.14, f32[8,256,256]{2,1,0:T(8,128)} %bitcast.8, f32[12,1,21]{2,1,0:T(1,128)} %bitcast.9, ...), custom_call_target="tpu_custom_call" | custom-call | tf_op jit(solution)/shard_map/pallas_call | solution.py:444
  36.3 2.7 %shard_map.105 = (f32[8,256,256]{2,1,0:T(8,128)}, f32[8,64,256]{2,1,0:T(8,128)}) custom-call(bf16[8,256,256]{2,1,0:T(8,128)(2,1)} %get-tuple-element.6.coadd_in, bf16[8,64,256]{2,1,0:T(8,128)(2,1)} %get-tuple-element.7.detect_in), custom_call_target="tpu_custom_call" | custom-call | tf_op jit(solution)/shard_map/pallas_call | solution.py:495

commit v3 on v2

--- a/solution.py
+++ b/solution.py
@@ -63,10 +63,7 @@
     stage,
     values,
     final,
-    det_stage,
     load_sem,
-    out_sem,
-    det_sem,
     meta_ssem,
     meta_rsem,
     x_ssem,
@@ -234,16 +231,6 @@
         r, sub = chunk_of(t)
         return pl.multiple_of(band_at(r) * rows + sub * part, part)
 
-    def coadd_copy(t):
-        return pltpu.make_async_copy(
-            final.at[t], coadd_ref.at[:, pl.ds(first_row(t), part), :], out_sem.at[t]
-        )
-
-    def detect_copy(sub):
-        return pltpu.make_async_copy(
-            det_stage.at[sub], detect_ref.at[:, pl.ds(pl.multiple_of(sub * part, part), part), :], det_sem.at[sub]
-        )
-
     def convolve(t):
         rows_in = pl.ds(first_row(t), window)
         for s in range(pieces):
@@ -314,11 +301,11 @@
             for p in range(PATCH_DEV):
                 value = sums[p] * jnp.broadcast_to(scale[:, p : p + 1], (block, side))
                 final[t, p, spot, :] = value.astype(BF16)
+                coadd_ref[p, pl.ds(pl.multiple_of(base + i * block, block), block), :] = value
                 values[lax.rem(t, 4), p, spot, :] = value
             return carry
 
         lax.fori_loop(0, part // block, some_rows, 0)
-        coadd_copy(t).start()
 
         @pl.when((r == 1) | ((r > 1) & (outer(r) == 1)))
         def _():
@@ -337,11 +324,10 @@
                 total = values[lax.rem(t, 4), p]
                 for hop, other in others:
                     total = total + z_recv[hop, other, p].astype(F32)
-                det_stage[sub, p] = total.astype(BF16)
+                detect_ref[p, pl.ds(pl.multiple_of(sub * part, part), part), :] = total
                 return carry
 
             lax.fori_loop(0, PATCH_DEV, add, 0)
-            detect_copy(sub).start()
 
     def forward(t, other):
         r = chunk_of(t)[0]
@@ -372,7 +358,7 @@
         def _():
             forward(t - 3, t - 2)
 
-    lag = 2
+    lag = 3
 
     def step(t, carry):
         @pl.when(t < chunks)
@@ -389,40 +375,28 @@
     lax.fori_loop(0, chunks + lag, step, 0)
 
     def finish(t, carry):
-        r, sub = chunk_of(t)
+        r = chunk_of(t)[0]
         for d in range(1, sky):
             sky_copy(t, d).wait_send()
-        coadd_copy(t).wait()
 
         @pl.when(r > 0)
         def _():
             band_copy(t, 1, final, 0).wait_send()
 
-        @pl.when(r == 0)
-        def _():
-            detect_copy(sub).wait()
-
         return carry
 
     lax.fori_loop(0, chunks, finish, 0)
 
 
-def widen(coadd_in, detect_in, coadd_out, detect_out, coadd_a, detect_a, coadd_b, detect_b, in_sem, out_sem):
-    pairs = ((coadd_in, coadd_a, coadd_b, coadd_out), (detect_in, detect_a, detect_b, detect_out))
-    loads, stores = [], []
-    for p in range(PATCH_DEV):
-        for which, (source, narrow, wide, dest) in enumerate(pairs):
-            loads.append(pltpu.make_async_copy(source.at[p], narrow.at[p], in_sem.at[which, p]))
-            stores.append(pltpu.make_async_copy(wide.at[p], dest.at[p], out_sem.at[which, p]))
-    for load in loads:
-        load.start()
-    for p in range(PATCH_DEV):
-        for which, (source, narrow, wide, dest) in enumerate(pairs):
-            loads[2 * p + which].wait()
-            wide[p] = narrow[p].astype(F32)
-            stores[2 * p + which].start()
-    for store in stores:
-        store.wait()
+def put(coadd_in, detect_in, coadd_out, detect_out, sem):
+    copies = [
+        pltpu.make_async_copy(coadd_in.at[p], coadd_out.at[p], sem.at[p]) for p in range(PATCH_DEV)
+    ]
+    copies.append(pltpu.make_async_copy(detect_in, detect_out, sem.at[PATCH_DEV]))
+    for copy in copies:
+        copy.start()
+    for copy in copies:
+        copy.wait()
 
 
 def per_device(
@@ -433,7 +407,7 @@
     sky, bands = lax.axis_size("sky"), lax.axis_size("band")
     cap = max(2, 2 * pieces // sky)
     rows = side // bands
-    part = min(rows, 32)
+    part = min(rows, 16)
     pad = -(-(taps // 2) // 16) * 16
     chunks = side // part
     meta_rows = -(-3 * cap // 8) * 8
@@ -444,11 +418,11 @@
     coadd, detection = pl.pallas_call(
         functools.partial(kernel, sizes),
         out_shape=(
-            jax.ShapeDtypeStruct((PATCH_DEV, side, side), BF16),
-            jax.ShapeDtypeStruct((PATCH_DEV, rows, side), BF16),
+            pltpu.VMEM((PATCH_DEV, side, side), F32),
+            pltpu.VMEM((PATCH_DEV, rows, side), F32),
         ),
         in_specs=[smem] * 5 + [hbm, vmem, vmem, vmem],
-        out_specs=(hbm, hbm),
+        out_specs=(vmem, vmem),
         scratch_shapes=[
             pltpu.VMEM((pieces, side, side), F32),
             pltpu.VMEM((pieces, side + 2 * pad, side), BF16),
@@ -467,10 +441,7 @@
             pltpu.VMEM((chunks, PATCH_DEV, part, side), BF16),
             pltpu.VMEM((4, PATCH_DEV, part, side), F32),
             pltpu.VMEM((chunks, PATCH_DEV, part, side), BF16),
-            pltpu.VMEM((rows // part, PATCH_DEV, part, side), BF16),
             pltpu.SemaphoreType.DMA((pieces,)),
-            pltpu.SemaphoreType.DMA((chunks,)),
-            pltpu.SemaphoreType.DMA((rows // part,)),
             pltpu.SemaphoreType.DMA((sky,)),
             pltpu.SemaphoreType.DMA((sky,)),
             pltpu.SemaphoreType.DMA((chunks, sky)),
@@ -492,23 +463,21 @@
         kernel_x,
         kernel_y,
     )
+    in_vmem = pltpu.MemorySpace.VMEM
     coadd, detection = pl.pallas_call(
-        widen,
+        put,
         out_shape=(
             jax.ShapeDtypeStruct(coadd.shape, F32),
             jax.ShapeDtypeStruct(detection.shape, F32),
         ),
-        in_specs=[hbm, hbm],
+        in_specs=[vmem, vmem],
         out_specs=(hbm, hbm),
-        scratch_shapes=[
-            pltpu.VMEM(coadd.shape, BF16),
-            pltpu.VMEM(detection.shape, BF16),
-            pltpu.VMEM(coadd.shape, F32),
-            pltpu.VMEM(detection.shape, F32),
-            pltpu.SemaphoreType.DMA((2, PATCH_DEV)),
-            pltpu.SemaphoreType.DMA((2, PATCH_DEV)),
-        ],
-    )(coadd, detection)
+        scratch_shapes=[pltpu.SemaphoreType.DMA((PATCH_DEV + 1,))],
+        compiler_params=pltpu.CompilerParams(vmem_limit_bytes=1024 * 1024),
+    )(
+        pltpu.with_memory_space_constraint(coadd, in_vmem),
+        pltpu.with_memory_space_constraint(detection, in_vmem),
+    )
     return coadd[None], detection
 
 

time: 39.4 us -> 36.8 us (0.934)
  Pallas kernels: 38.4 us -> 36 us
    pallas_call x2, Pallas kernels: 38.4 us -> 36 us  [the longest x1 34.4 us: per_device(): pl.pallas_call(functools.partial(kernel, sizes), out_shape=(pltpu.VMEM((P...]
where the time goes in v3:
time: 36.8 us; the launch traced here: 36.6 us
  Pallas kernels  36 us (98%)
  between operations  0.64 us (2%)
    pallas_call x1, Pallas kernels, per_device(): pl.pallas_call(functools.partial(kernel, sizes), out_shape=(pltpu.VMEM((P...  34.4 us
    pallas_call x1, Pallas kernels, per_device(): pl.pallas_call(put, out_shape=(jax.ShapeDtypeStruct(coadd.shape, F32), ja...  1.56 us

profile of v3, /device:TPU:0, one launch (start us, length us, event | category | flops | bytes accessed | tf_op | source)
XLA Modules:
  0.0 36.6 jit_solution(16764517312742179565)
XLA Ops:
  0.6 34.4 %shard_map.104 = (f32[8,256,256]{2,1,0:T(8,128)S(1)}, f32[8,64,256]{2,1,0:T(8,128)S(1)}) custom-call(s32[8]{0:T(128)} %bitcast.10, s32[8]{0:T(128)} %bitcast.11, s32[8]{0:T(128)} %bitcast.12, s32[8]{0:T(128)} %bitcast.13, f32[12]{0:T(128)} %bitcast.14, f32[8,256,256]{2,1,0:T(8,128)} %bitcast.8, f32[12,1,21]{2,1,0:T(1,128)} %bitcast.9, ...), custom_call_target="tpu_custom_call" | custom-call | tf_op jit(solution)/shard_map/pallas_call | solution.py:418
  35.0 1.6 %shard_map.105 = (f32[8,256,256]{2,1,0:T(8,128)}, f32[8,64,256]{2,1,0:T(8,128)}) custom-call(f32[8,256,256]{2,1,0:T(8,128)S(1)} %get-tuple-element.6.coadd_in, f32[8,64,256]{2,1,0:T(8,128)S(1)} %get-tuple-element.7.detect_in), custom_call_target="tpu_custom_call" | custom-call | tf_op jit(solution)/shard_map/pallas_call | solution.py:467

commit v4 on v3

--- a/solution.py
+++ b/solution.py
@@ -178,8 +178,13 @@
         row = jnp.broadcast_to(bases[pl.ds(basis + k, 1), :], (wide, wide))
         ring = pltpu.roll(row, 0, 1, stride=1, stride_axis=0)
         on = jnp.where(jnp.abs(ring_row - ring_col) <= half, ring, 0.0).astype(BF16)
-        below = jnp.where(ring_col - ring_row >= wide - half, ring, 0.0).astype(BF16)
-        above = jnp.where(ring_row - ring_col >= wide - half, ring, 0.0).astype(BF16)
+        edge = -(-half // 16) * 16
+        rest = jnp.zeros((wide - edge, wide), BF16)
+        top = jnp.where(ring_col[:edge] - ring_row[:edge] >= wide - half, ring[:edge], 0.0)
+        below = jnp.concatenate([top.astype(BF16), rest], axis=0)
+        low = wide - edge
+        end = jnp.where(ring_row[low:] - ring_col[low:] >= wide - half, ring[low:], 0.0)
+        above = jnp.concatenate([rest, end.astype(BF16)], axis=0)
         none = jnp.zeros((wide, wide), BF16)
         pick = {0: on, 1: below, -1: above}
         for i in range(blocks):
@@ -188,7 +193,7 @@
                 across[spot, j * wide : (j + 1) * wide] = pick.get(i - j, none)
         return carry
 
-    lax.fori_loop(0, basis, make_tables, 0)
+    lax.fori_loop(0, basis, make_tables, 0, unroll=3)
 
     row_ids = lax.broadcasted_iota(jnp.int32, (side, side), 0)
     for s in range(pieces):

time: 36.8 us -> 36 us (0.978)
  Pallas kernels: 36 us -> 35.2 us
    pallas_call x1, Pallas kernels: 34.4 us -> 33.6 us  [per_device(): pl.pallas_call(functools.partial(kernel, sizes), out_shape=(pltpu.VMEM((P...]
where the time goes in v4:
time: 36 us; the launch traced here: 35.8 us
  Pallas kernels  35.2 us (98%)
  between operations  0.64 us (2%)
    pallas_call x1, Pallas kernels, per_device(): pl.pallas_call(functools.partial(kernel, sizes), out_shape=(pltpu.VMEM((P...  33.6 us
    pallas_call x1, Pallas kernels, per_device(): pl.pallas_call(put, out_shape=(jax.ShapeDtypeStruct(coadd.shape, F32), ja...  1.56 us

profile of v4, /device:TPU:0, one launch (start us, length us, event | category | flops | bytes accessed | tf_op | source)
XLA Modules:
  0.0 35.8 jit_solution(11189318002099398430)
XLA Ops:
  0.6 33.6 %shard_map.104 = (f32[8,256,256]{2,1,0:T(8,128)S(1)}, f32[8,64,256]{2,1,0:T(8,128)S(1)}) custom-call(s32[8]{0:T(128)} %bitcast.10, s32[8]{0:T(128)} %bitcast.11, s32[8]{0:T(128)} %bitcast.12, s32[8]{0:T(128)} %bitcast.13, f32[12]{0:T(128)} %bitcast.14, f32[8,256,256]{2,1,0:T(8,128)} %bitcast.8, f32[12,1,21]{2,1,0:T(1,128)} %bitcast.9, ...), custom_call_target="tpu_custom_call" | custom-call | tf_op jit(solution)/shard_map/pallas_call | solution.py:423
  34.3 1.6 %shard_map.105 = (f32[8,256,256]{2,1,0:T(8,128)}, f32[8,64,256]{2,1,0:T(8,128)}) custom-call(f32[8,256,256]{2,1,0:T(8,128)S(1)} %get-tuple-element.6.coadd_in, f32[8,64,256]{2,1,0:T(8,128)S(1)} %get-tuple-element.7.detect_in), custom_call_target="tpu_custom_call" | custom-call | tf_op jit(solution)/shard_map/pallas_call | solution.py:472

commit v5 on v3

--- a/solution.py
+++ b/solution.py
@@ -89,6 +89,12 @@
     def sky_at(d):
         return lax.rem(me + d, sky)
 
+    loads = [
+        pltpu.make_async_copy(patches_ref.at[s], raw.at[s], load_sem.at[s]) for s in range(pieces)
+    ]
+    for load in loads:
+        load.start()
+
     barrier = pltpu.get_barrier_semaphore()
     for d in range(1, sky):
         pl.semaphore_signal(barrier, inc=1, device_id={"sky": sky_at(d)}, device_id_type=MESH)
@@ -115,11 +121,39 @@
             greet()
             greeted = greeted + 1
 
-    loads = [
-        pltpu.make_async_copy(patches_ref.at[s], raw.at[s], load_sem.at[s]) for s in range(pieces)
-    ]
-    for load in loads:
-        load.start()
+    wide = bases.shape[1]
+    taps_at = lax.broadcasted_iota(jnp.int32, (taps, wide), 0) - half
+    lanes = lax.broadcasted_iota(jnp.int32, (taps, wide), 1)
+    for start, ref, away in ((0, ky_ref, pad + taps_at), (basis, kx_ref, -taps_at)):
+        place = (lanes == jnp.where(away < 0, away + wide, away)).astype(BF16)
+        bases[start : start + basis, :] = jnp.dot(ref[...], place, preferred_element_type=F32)
+    ring_row = lax.broadcasted_iota(jnp.int32, (wide, wide), 0)
+    ring_col = lax.broadcasted_iota(jnp.int32, (wide, wide), 1)
+    blocks = side // wide
+
+    def make_tables(k, carry):
+        row = jnp.broadcast_to(bases[pl.ds(k, 1), :], (part, wide))
+        shifted = pltpu.roll(row, 0, 1, stride=1, stride_axis=0)
+        down[pl.ds(pl.multiple_of(k * part, part), part), :] = shifted[:, :window].astype(BF16)
+        row = jnp.broadcast_to(bases[pl.ds(basis + k, 1), :], (wide, wide))
+        ring = pltpu.roll(row, 0, 1, stride=1, stride_axis=0)
+        on = jnp.where(jnp.abs(ring_row - ring_col) <= half, ring, 0.0).astype(BF16)
+        edge = -(-half // 16) * 16
+        rest = jnp.zeros((wide - edge, wide), BF16)
+        top = jnp.where(ring_col[:edge] - ring_row[:edge] >= wide - half, ring[:edge], 0.0)
+        below = jnp.concatenate([top.astype(BF16), rest], axis=0)
+        low = wide - edge
+        end = jnp.where(ring_row[low:] - ring_col[low:] >= wide - half, ring[low:], 0.0)
+        above = jnp.concatenate([rest, end.astype(BF16)], axis=0)
+        none = jnp.zeros((wide, wide), BF16)
+        pick = {0: on, 1: below, -1: above}
+        for i in range(blocks):
+            for j in range(blocks):
+                spot = pl.ds(pl.multiple_of(k * side + i * wide, wide), wide)
+                across[spot, j * wide : (j + 1) * wide] = pick.get(i - j, none)
+        return carry
+
+    lax.fori_loop(0, basis, make_tables, 0, unroll=3)
 
     owners = [owner_ref[s] for s in range(pieces)]
     ranks = []
@@ -161,35 +195,6 @@
         ).astype(F32)
     meta_recv[me] = meta_send[me]
 
-    wide = bases.shape[1]
-    taps_at = lax.broadcasted_iota(jnp.int32, (taps, wide), 0) - half
-    lanes = lax.broadcasted_iota(jnp.int32, (taps, wide), 1)
-    for start, ref, away in ((0, ky_ref, pad + taps_at), (basis, kx_ref, -taps_at)):
-        place = (lanes == jnp.where(away < 0, away + wide, away)).astype(BF16)
-        bases[start : start + basis, :] = jnp.dot(ref[...], place, preferred_element_type=F32)
-    ring_row = lax.broadcasted_iota(jnp.int32, (wide, wide), 0)
-    ring_col = lax.broadcasted_iota(jnp.int32, (wide, wide), 1)
-    blocks = side // wide
-
-    def make_tables(k, carry):
-        row = jnp.broadcast_to(bases[pl.ds(k, 1), :], (part, wide))
-        shifted = pltpu.roll(row, 0, 1, stride=1, stride_axis=0)
-        down[pl.ds(pl.multiple_of(k * part, part), part), :] = shifted[:, :window].astype(BF16)
-        row = jnp.broadcast_to(bases[pl.ds(basis + k, 1), :], (wide, wide))
-        ring = pltpu.roll(row, 0, 1, stride=1, stride_axis=0)
-        on = jnp.where(jnp.abs(ring_row - ring_col) <= half, ring, 0.0).astype(BF16)
-        below = jnp.where(ring_col - ring_row >= wide - half, ring, 0.0).astype(BF16)
-        above = jnp.where(ring_row - ring_col >= wide - half, ring, 0.0).astype(BF16)
-        none = jnp.zeros((wide, wide), BF16)
-        pick = {0: on, 1: below, -1: above}
-        for i in range(blocks):
-            for j in range(blocks):
-                spot = pl.ds(pl.multiple_of(k * side + i * wide, wide), wide)
-                across[spot, j * wide : (j + 1) * wide] = pick.get(i - j, none)
-        return carry
-
-    lax.fori_loop(0, basis, make_tables, 0)
-
     row_ids = lax.broadcasted_iota(jnp.int32, (side, side), 0)
     for s in range(pieces):
         tiles[s, 0:pad, :] = jnp.zeros((pad, side), BF16)
@@ -360,20 +365,6 @@
 
     lag = 3
 
-    def step(t, carry):
-        @pl.when(t < chunks)
-        def _():
-            convolve(t)
-
-        @pl.when(t >= lag)
-        def _():
-            collect(t - lag)
-            forwards(t - lag)
-
-        return carry
-
-    lax.fori_loop(0, chunks + lag, step, 0)
-
     def finish(t, carry):
         r = chunk_of(t)[0]
         for d in range(1, sky):
@@ -385,7 +376,27 @@
 
         return carry
 
-    lax.fori_loop(0, chunks, finish, 0)
+    held = 6
+
+    def step(t, carry):
+        @pl.when(t < chunks)
+        def _():
+            convolve(t)
+
+        @pl.when(t >= lag)
+        def _():
+            collect(t - lag)
+            forwards(t - lag)
+
+        @pl.when(t >= lag + held)
+        def _():
+            finish(t - lag - held, 0)
+
+        return carry
+
+    lax.fori_loop(0, chunks + lag, step, 0)
+
+    lax.fori_loop(max(0, chunks - held), chunks, finish, 0)
 
 
 def put(coadd_in, detect_in, coadd_out, detect_out, sem):

time: 36.8 us -> 35.6 us (0.967)
  Pallas kernels: 36 us -> 34.8 us
    pallas_call x1, Pallas kernels: 34.4 us -> 33.2 us  [per_device(): pl.pallas_call(functools.partial(kernel, sizes), out_shape=(pltpu.VMEM((P...]
where the time goes in v5:
time: 35.6 us; the launch traced here: 35.4 us
  Pallas kernels  34.8 us (98%)
  between operations  0.64 us (2%)
    pallas_call x1, Pallas kernels, per_device(): pl.pallas_call(functools.partial(kernel, sizes), out_shape=(pltpu.VMEM((P...  33.2 us
    pallas_call x1, Pallas kernels, per_device(): pl.pallas_call(put, out_shape=(jax.ShapeDtypeStruct(coadd.shape, F32), ja...  1.56 us

profile of v5, /device:TPU:0, one launch (start us, length us, event | category | flops | bytes accessed | tf_op | source)
XLA Modules:
  0.0 35.4 jit_solution(8795226468231453341)
XLA Ops:
  0.6 33.2 %shard_map.104 = (f32[8,256,256]{2,1,0:T(8,128)S(1)}, f32[8,64,256]{2,1,0:T(8,128)S(1)}) custom-call(s32[8]{0:T(128)} %bitcast.10, s32[8]{0:T(128)} %bitcast.11, s32[8]{0:T(128)} %bitcast.12, s32[8]{0:T(128)} %bitcast.13, f32[12]{0:T(128)} %bitcast.14, f32[8,256,256]{2,1,0:T(8,128)} %bitcast.8, f32[12,1,21]{2,1,0:T(1,128)} %bitcast.9, ...), custom_call_target="tpu_custom_call" | custom-call | tf_op jit(solution)/shard_map/pallas_call | solution.py:429
  33.9 1.6 %shard_map.105 = (f32[8,256,256]{2,1,0:T(8,128)}, f32[8,64,256]{2,1,0:T(8,128)}) custom-call(f32[8,256,256]{2,1,0:T(8,128)S(1)} %get-tuple-element.6.coadd_in, f32[8,64,256]{2,1,0:T(8,128)S(1)} %get-tuple-element.7.detect_in), custom_call_target="tpu_custom_call" | custom-call | tf_op jit(solution)/shard_map/pallas_call | solution.py:478

commit v6 on v5

--- a/solution.py
+++ b/solution.py
@@ -153,7 +153,7 @@
                 across[spot, j * wide : (j + 1) * wide] = pick.get(i - j, none)
         return carry
 
-    lax.fori_loop(0, basis, make_tables, 0, unroll=3)
+    lax.fori_loop(0, basis, make_tables, 0, unroll=7)
 
     owners = [owner_ref[s] for s in range(pieces)]
     ranks = []

time: 35.6 us -> 35.5 us (level)
  no operation moved by 1% of the time
where the time goes in v6:
time: 35.5 us; the launch traced here: 35.3 us
  Pallas kernels  34.7 us (98%)
  between operations  0.64 us (2%)
    pallas_call x1, Pallas kernels, per_device(): pl.pallas_call(functools.partial(kernel, sizes), out_shape=(pltpu.VMEM((P...  33.1 us
    pallas_call x1, Pallas kernels, per_device(): pl.pallas_call(put, out_shape=(jax.ShapeDtypeStruct(coadd.shape, F32), ja...  1.56 us

profile of v6, /device:TPU:0, one launch (start us, length us, event | category | flops | bytes accessed | tf_op | source)
XLA Modules:
  0.0 35.3 jit_solution(13499289087676373074)
XLA Ops:
  0.6 33.1 %shard_map.104 = (f32[8,256,256]{2,1,0:T(8,128)S(1)}, f32[8,64,256]{2,1,0:T(8,128)S(1)}) custom-call(s32[8]{0:T(128)} %bitcast.10, s32[8]{0:T(128)} %bitcast.11, s32[8]{0:T(128)} %bitcast.12, s32[8]{0:T(128)} %bitcast.13, f32[12]{0:T(128)} %bitcast.14, f32[8,256,256]{2,1,0:T(8,128)} %bitcast.8, f32[12,1,21]{2,1,0:T(1,128)} %bitcast.9, ...), custom_call_target="tpu_custom_call" | custom-call | tf_op jit(solution)/shard_map/pallas_call | solution.py:429
  33.8 1.6 %shard_map.105 = (f32[8,256,256]{2,1,0:T(8,128)}, f32[8,64,256]{2,1,0:T(8,128)}) custom-call(f32[8,256,256]{2,1,0:T(8,128)S(1)} %get-tuple-element.6.coadd_in, f32[8,64,256]{2,1,0:T(8,128)S(1)} %get-tuple-element.7.detect_in), custom_call_target="tpu_custom_call" | custom-call | tf_op jit(solution)/shard_map/pallas_call | solution.py:478

commit v7 on v5

--- a/solution.py
+++ b/solution.py
@@ -90,7 +90,13 @@
         return lax.rem(me + d, sky)
 
     loads = [
-        pltpu.make_async_copy(patches_ref.at[s], raw.at[s], load_sem.at[s]) for s in range(pieces)
+        pltpu.make_async_copy(
+            patches_ref.at[s, pl.ds(i * side // 2, side // 2)],
+            raw.at[s, pl.ds(i * side // 2, side // 2)],
+            load_sem.at[2 * s + i],
+        )
+        for s in range(pieces)
+        for i in range(2)
     ]
     for load in loads:
         load.start()
@@ -199,7 +205,8 @@
     for s in range(pieces):
         tiles[s, 0:pad, :] = jnp.zeros((pad, side), BF16)
         tiles[s, pad + side : side + 2 * pad, :] = jnp.zeros((pad, side), BF16)
-        loads[s].wait()
+        loads[2 * s].wait()
+        loads[2 * s + 1].wait()
         tiles[s, pad : pad + side, :] = jnp.where(row_ids < valid_ref[s], raw[s], 0.0).astype(BF16)
 
     def meta_copy(d):
@@ -452,7 +459,7 @@
             pltpu.VMEM((chunks, PATCH_DEV, part, side), BF16),
             pltpu.VMEM((4, PATCH_DEV, part, side), F32),
             pltpu.VMEM((chunks, PATCH_DEV, part, side), BF16),
-            pltpu.SemaphoreType.DMA((pieces,)),
+            pltpu.SemaphoreType.DMA((2 * pieces,)),
             pltpu.SemaphoreType.DMA((sky,)),
             pltpu.SemaphoreType.DMA((sky,)),
             pltpu.SemaphoreType.DMA((chunks, sky)),

time: 35.6 us -> 35.7 us (level)
  no operation moved by 1% of the time
where the time goes in v7:
time: 35.7 us; the launch traced here: 35.5 us
  Pallas kernels  34.9 us (98%)
  between operations  0.64 us (2%)
    pallas_call x1, Pallas kernels, per_device(): pl.pallas_call(functools.partial(kernel, sizes), out_shape=(pltpu.VMEM((P...  33.3 us
    pallas_call x1, Pallas kernels, per_device(): pl.pallas_call(put, out_shape=(jax.ShapeDtypeStruct(coadd.shape, F32), ja...  1.56 us

profile of v7, /device:TPU:0, one launch (start us, length us, event | category | flops | bytes accessed | tf_op | source)
XLA Modules:
  0.0 35.5 jit_solution(14719990811563952944)
XLA Ops:
  0.6 33.3 %shard_map.104 = (f32[8,256,256]{2,1,0:T(8,128)S(1)}, f32[8,64,256]{2,1,0:T(8,128)S(1)}) custom-call(s32[8]{0:T(128)} %bitcast.10, s32[8]{0:T(128)} %bitcast.11, s32[8]{0:T(128)} %bitcast.12, s32[8]{0:T(128)} %bitcast.13, f32[12]{0:T(128)} %bitcast.14, f32[8,256,256]{2,1,0:T(8,128)} %bitcast.8, f32[12,1,21]{2,1,0:T(1,128)} %bitcast.9, ...), custom_call_target="tpu_custom_call" | custom-call | tf_op jit(solution)/shard_map/pallas_call | solution.py:436
  34.0 1.6 %shard_map.105 = (f32[8,256,256]{2,1,0:T(8,128)}, f32[8,64,256]{2,1,0:T(8,128)}) custom-call(f32[8,256,256]{2,1,0:T(8,128)S(1)} %get-tuple-element.6.coadd_in, f32[8,64,256]{2,1,0:T(8,128)S(1)} %get-tuple-element.7.detect_in), custom_call_target="tpu_custom_call" | custom-call | tf_op jit(solution)/shard_map/pallas_call | solution.py:485
